TPU v7x, 256 devices: a whole 4x4x8 slice. The times are simulated.
256 devices in a mesh: row: 32 (over x, y, core), col: 8 (over z).
Axes of the slice: x: 4, y: 4, z: 8, core: 2. Of those that a mesh axis runs over, the one named last changes fastest.
Arguments:
- test_kernel: float32 [65536, 4096], P('row', 'col'), may hold values from -6 to 6
- first_panel: float32 [65536, 512], P('row', 'col'), may hold values from -0.25 to 0.25
- second_panel: float32 [65536, 512], P('row', 'col'), may hold values from -0.25 to 0.25
- first_inverse: float32 [512, 512], replicated, may hold values from -0.15 to 1.5, as said below
- second_inverse: float32 [512, 512], replicated, may hold values from -0.15 to 1.5, as said below
Outputs:
- solution: float32 [65536, 4096], P('row', 'col')
Inputs may be any that keep to these rules, and one draw needn't show every extreme that they name: `first_inverse`: lower triangular: zeros above the diagonal, diagonal entries positive. `second_inverse`: lower triangular: zeros above the diagonal, diagonal entries positive.
All inputs are finite; a program needn't handle non-finite values.
Results may differ from a plain program's by a relative error of at most 0.000075.
Values sent between devices are 32-bit elements; how exact they have to be, the bound alone decides.
A program may use at most 64 MiB of HBM per device.

v0:
```python
import jax
import jax.numpy as jnp
from jax import lax
from jax.sharding import PartitionSpec as P


def broadcast(value, axis, source):
    kept = jnp.where(lax.axis_index(axis) == source, value, 0).astype(value.dtype)
    return lax.psum(kept, axis)


def product(left, right):
    return jnp.dot(left, right, precision=lax.Precision.HIGHEST, preferred_element_type=jnp.float32)


def folding(solved, piece):
    return product(piece, solved)


def per_device(test_kernel, first_panel, second_panel, first_inverse, second_inverse):
    block = first_inverse.shape[0]
    position = lax.axis_index("row")
    first_rows = broadcast(test_kernel[:block], "row", 0)
    first_solved = product(first_inverse, first_rows)
    update_one = folding(first_solved, lax.all_gather(first_panel, "col", axis=1, tiled=True))
    partial_value = test_kernel - update_one
    second_rows = broadcast(partial_value[:block], "row", 1)
    second_solved = product(second_inverse, second_rows)
    update_two = folding(second_solved, lax.all_gather(second_panel, "col", axis=1, tiled=True))
    final = partial_value - update_two
    leading_final = jnp.where(
        position == 0, first_solved, jnp.where(position == 1, second_solved, final[:block])
    )
    return final.at[:block].set(leading_final)


def solution(mesh):
    in_specs = (P("row", "col"), P("row", "col"), P("row", "col"), P(), P())
    out_specs = P("row", "col")
    return jax.shard_map(
        per_device, mesh=mesh, in_specs=in_specs, out_specs=out_specs, check_vma=False
    )
```

profile of v0, /device:TPU:1, one launch (start us, length us, event | category | flops | bytes accessed | tf_op | source)
XLA Modules:
  0.0 296.1 jit_solution(15105920552222023866)
XLA Ops:
  7.4 0.0 copy-start
  7.4 0.0 all-reduce.3.cloned.1.call-start
  7.4 5.4 %copy.7 = f32[2048,512]{0,1:T(8,128)} copy(f32[2048,512]{1,0:T(8,128)} %param.7) | data formatting | bytes 8388608 | tf_op args[0]
  12.8 2.3 slice_select_fusion.2
  15.1 0.0 all-reduce.3.cloned.1.call-update
  15.1 0.0 all-gather.3.cloned.1.call-start
  15.2 0.5 all-gather.3.cloned.1.call-update
  15.7 0.0 all-reduce.5.cloned.1.call-start
  15.8 119.1 %all-reduce.3.cloned.1.call-done = f32[512,512]{0,1:T(8,128)} async-done(((f32[512,512]{0,1:T(8,128)}), f32[512,512]{0,1:T(8,128)}) %all-reduce.3.cloned.1.call-update) | async-done | bytes 1048592 | tf_op jit(solution)/shard_map/psum | solution.py:9
  134.9 0.0 copy-done
  134.9 3.1 %fusion.2 = f32[512,512]{1,0:T(8,128)S(1)} fusion(f32[512,512]{0,1:T(8,128)} %all-reduce.3.cloned.1.call-done, f32[512,512]{1,0:T(8,128)S(1)} %copy-done), kind=kOutput, calls=%fused_computation.7 | convolution fusion | flops 1610612736 | bytes 3145728 | tf_op jit(solution)/shard_map/dot_general | solution.py:13
  138.0 0.0 all-gather.3.cloned.1.call-done
  138.0 9.4 %bitcast_subtract_fusion.1 = f32[2048,512]{0,1:T(8,128)S(1)} fusion(f32[2048,512]{0,1:T(8,128)} %copy.7, f32[512,512]{1,0:T(8,128)S(1)} %fusion.2, f32[2048,512]{0,1:T(8,128)} %all-gather.3.cloned.1.call-done), kind=kOutput, calls=%fused_computation.1 | convolution fusion | flops 6443499520 | bytes 13631488 | tf_op jit(solution)/shard_map/dot_general | solution.py:13
  147.5 0.0 copy-start.1
  147.5 2.0 copy-done.1
  149.5 1.1 slice_select_fusion.1
  150.6 0.0 all-reduce.5.cloned.1.call-update
  150.6 0.2 all-gather.5.cloned.1.call-start
  150.9 0.4 all-gather.5.cloned.1.call-update
  151.2 115.2 %all-reduce.5.cloned.1.call-done = f32[512,512]{0,1:T(8,128)} async-done(((f32[512,512]{0,1:T(8,128)}), f32[512,512]{0,1:T(8,128)}) %all-reduce.5.cloned.1.call-update) | async-done | bytes 1048592 | tf_op jit(solution)/shard_map/psum | solution.py:9
  266.5 3.4 %fusion.3 = f32[512,512]{1,0:T(8,128)S(1)} fusion(f32[512,512]{0,1:T(8,128)} %all-reduce.5.cloned.1.call-done, f32[512,512]{1,0:T(8,128)} %param.11), kind=kOutput, calls=%fused_computation.8 | convolution fusion | flops 1610612736 | bytes 3145728 | tf_op jit(solution)/shard_map/dot_general | solution.py:13
  269.9 0.0 all-gather.5.cloned.1.call-done
  269.9 10.8 %bitcast_subtract_fusion = f32[2048,512]{0,1:T(8,128)} fusion(f32[2048,512]{0,1:T(8,128)} %copy-done.1, f32[512,512]{1,0:T(8,128)S(1)} %fusion.3, f32[2048,512]{0,1:T(8,128)} %all-gather.5.cloned.1.call-done), kind=kOutput, calls=%fused_computation | convolution fusion | flops 6443499520 | bytes 13631488 | tf_op jit(solution)/shard_map/dot_general | solution.py:13
  280.7 2.6 fusion.1
  283.3 5.3 %copy.8 = f32[2048,512]{1,0:T(8,128)} copy(f32[2048,512]{0,1:T(8,128)} %fusion.1) | data formatting | bytes 8388608 | tf_op jit(solution)/shard_map/scatter | solution.py:34
Async XLA Ops:
  7.4 127.6 %copy-start = (f32[512,512]{1,0:T(8,128)S(1)}, f32[512,512]{1,0:T(8,128)}, u32[]{:S(2)}) copy-start(f32[512,512]{1,0:T(8,128)} %param.10) | copy-start | bytes 3145732
  7.4 127.5 %all-reduce.3.cloned.1.call-start = ((), (), s32[]{:S(2)}) async-start(), calls=%async_computation | async-start | bytes 2097152 | tf_op jit(solution)/shard_map/psum | solution.py:9
  15.1 122.9 %all-gather.3.cloned.1.call-start = ((), (), s32[]{:S(2)}) async-start(), calls=%async_computation.1 | async-start | bytes 4718592 | tf_op jit(solution)/shard_map/all_gather | solution.py:25
  15.7 250.7 %all-reduce.5.cloned.1.call-start = ((), (), s32[]{:S(2)}) async-start(), calls=%async_computation.2 | async-start | bytes 2097152 | tf_op jit(solution)/shard_map/psum | solution.py:9
  147.5 2.0 copy-start.1
  150.6 119.3 %all-gather.5.cloned.1.call-start = ((), (), s32[]{:S(2)}) async-start(), calls=%async_computation.3 | async-start | bytes 4718592 | tf_op jit(solution)/shard_map/all_gather | solution.py:29
Sparse Core Ops, SparseCore 0:
  15.3 119.6 all-reduce.2
  150.8 115.6 all-reduce.4
Sparse Core Ops, SparseCore 1:
  17.5 58.4 all-gather.2
  152.9 54.4 all-gather.4
where the time goes:
time: 296 us
  waiting for transfers between devices  235 us (79%)
  matrix products  26.7 us (9%)
  between operations  14.9 us (5%)
  local copies, waits for them, and re-layouts  12.8 us (4%)
  other arithmetic  6.08 us (2%)
    psum x2, waiting for transfers between devices, broadcast(): return lax.psum(kept, axis)  234 us
    dot_general x4, matrix products, product(): jnp.dot(left, right, precision=lax.Precision.HIGHEST, preferred_element_t...  26.7 us
    unnamed x5, local copies, waits for them, and re-layouts  7.44 us
  transfers between devices with their start and end apart: 4, of which 2 were waited for; matrix products, arithmetic and copies ran while one was open for 2% of the time, Pallas kernels for 0%

commit v1 on v0

--- a/solution.py
+++ b/solution.py
@@ -6,7 +6,7 @@
 
 def broadcast(value, axis, source):
     kept = jnp.where(lax.axis_index(axis) == source, value, 0).astype(value.dtype)
-    return lax.psum(kept, axis)
+    return jnp.sum(lax.all_gather(kept, axis), axis=0)
 
 
 def product(left, right):

time: 296 us -> 405 us (1.37)
  local copies, waits for them, and re-layouts: 12.8 us -> 77.8 us
  waiting for transfers between devices: 235 us -> 272 us
  other arithmetic: 6.08 us -> 16.8 us
    all_gather x0 -> x2, waiting for transfers between devices: none -> 240 us  [broadcast(): return jnp.sum(lax.all_gather(kept, axis), axis=0)]
    psum x2 -> x0, waiting for transfers between devices: 234 us -> none  [broadcast(): return lax.psum(kept, axis)]
    unnamed x5 -> x11, local copies, waits for them, and re-layouts: 7.44 us -> 72.5 us
    all_gather x1, waiting for transfers between devices: 0.03 us -> 15.9 us  [per_device(): lax.all_gather(first_panel, 'col', axis=1, tiled=True)]
    all_gather x1, waiting for transfers between devices: 0.03 us -> 15.7 us  [per_device(): lax.all_gather(second_panel, 'col', axis=1, tiled=True)]
    reduce_sum x0 -> x2, other arithmetic: none -> 10.7 us  [broadcast(): return jnp.sum(lax.all_gather(kept, axis), axis=0)]
  transfers between devices with their start and end apart: 4 -> 4, of which waited for: 2 -> 4; matrix products, arithmetic and copies ran while one was open for 2% -> 20% of each run, Pallas kernels for 0% -> 0%
where the time goes in v1:
time: 405 us; the launch traced here: 404 us
  waiting for transfers between devices  272 us (67%)
  local copies, waits for them, and re-layouts  77.8 us (19%)
  matrix products  23.9 us (6%)
  other arithmetic  16.8 us (4%)
  between operations  13.2 us (3%)
    all_gather x2, waiting for transfers between devices, broadcast(): return jnp.sum(lax.all_gather(kept, axis), axis=0)  240 us
    unnamed x11, local copies, waits for them, and re-layouts  72.5 us
    dot_general x4, matrix products, product(): jnp.dot(left, right, precision=lax.Precision.HIGHEST, preferred_element_t...  23.9 us
    all_gather x1, waiting for transfers between devices, per_device(): lax.all_gather(first_panel, 'col', axis=1, tiled=True)  15.9 us
    all_gather x1, waiting for transfers between devices, per_device(): lax.all_gather(second_panel, 'col', axis=1, tiled=True)  15.7 us
    reduce_sum x2, other arithmetic, broadcast(): return jnp.sum(lax.all_gather(kept, axis), axis=0)  10.7 us
  transfers between devices with their start and end apart: 4, of which 4 were waited for; matrix products, arithmetic and copies ran while one was open for 20% of the time, Pallas kernels for 0%

profile of v1, /device:TPU:1, one launch (start us, length us, event | category | flops | bytes accessed | tf_op | source)
XLA Modules:
  0.0 404.4 jit_solution(6480048097025427625)
XLA Ops:
  6.5 0.0 copy-start
  6.5 0.0 all-gather.11.cloned.1.call-start
  6.5 5.4 %copy.10 = f32[2048,512]{0,1:T(8,128)} copy(f32[2048,512]{1,0:T(8,128)} %param.7) | data formatting | bytes 8388608 | tf_op args[0]
  12.0 2.3 slice_select_fusion.2
  14.3 0.0 all-gather.11.cloned.1.call-update
  14.3 0.0 all-gather.7.cloned.1.call-start
  14.3 0.7 all-gather.7.cloned.1.call-update
  15.0 0.0 all-gather.13.cloned.1.call-start
  15.1 122.4 %all-gather.11.cloned.1.call-done = f32[16384,512]{0,1:T(8,128)} async-done(((f32[512,512]{0,1:T(8,128)}), f32[16384,512]{0,1:T(8,128)}) %all-gather.11.cloned.1.call-update) | async-done | bytes 33554448 | tf_op jit(solution)/shard_map/all_gather | solution.py:9
  137.5 32.5 %copy.12 = f32[64,8,32,512]{3,2,1,0:T(8,128)S(1)} copy(f32[64,8,32,512]{3,1,2,0:T(8,128)} %bitcast.26) | data formatting | bytes 67108864
  170.0 5.4 %bitcast_reduce_fusion.1 = f32[512,512]{0,1:T(8,128)S(1)} fusion(f32[64,8,32,512]{3,2,1,0:T(8,128)S(1)} %copy.12), kind=kLoop, calls=%fused_computation.1 | loop fusion | flops 8126464 | bytes 34603008 | tf_op jit(solution)/shard_map/reduce_sum | solution.py:9
  175.3 0.0 copy-done
  175.4 1.9 fusion.2
  177.2 15.9 %all-gather.7.cloned.1.call-done = f32[2048,512]{0,1:T(8,128)} async-done(((f32[2048,64]{0,1:T(8,128)}), f32[2048,512]{0,1:T(8,128)}) %all-gather.7.cloned.1.call-update) | async-done | bytes 4194320 | tf_op jit(solution)/shard_map/all_gather | solution.py:25
  193.1 9.4 %bitcast_subtract_fusion.1 = f32[2048,512]{0,1:T(8,128)S(1)} fusion(f32[2048,512]{0,1:T(8,128)} %copy.10, f32[512,512]{1,0:T(8,128)S(1)} %fusion.2, f32[2048,512]{0,1:T(8,128)} %all-gather.7.cloned.1.call-done), kind=kOutput, calls=%fused_computation.3 | convolution fusion | flops 6443499520 | bytes 13631488 | tf_op jit(solution)/shard_map/dot_general | solution.py:13
  202.5 0.0 copy-start.2
  202.5 2.0 copy-done.2
  204.5 1.1 slice_select_fusion.1
  205.6 0.0 all-gather.13.cloned.1.call-update
  205.6 0.2 all-gather.9.cloned.1.call-start
  205.9 0.3 all-gather.9.cloned.1.call-update
  206.2 117.4 %all-gather.13.cloned.1.call-done = f32[16384,512]{0,1:T(8,128)} async-done(((f32[512,512]{0,1:T(8,128)}), f32[16384,512]{0,1:T(8,128)}) %all-gather.13.cloned.1.call-update) | async-done | bytes 33554448 | tf_op jit(solution)/shard_map/all_gather | solution.py:9
  323.6 32.5 %copy.13 = f32[64,8,32,512]{3,2,1,0:T(8,128)S(1)} copy(f32[64,8,32,512]{3,1,2,0:T(8,128)} %bitcast.27) | data formatting | bytes 67108864
  356.1 0.0 copy-start.3
  356.1 5.4 %bitcast_reduce_fusion = f32[512,512]{0,1:T(8,128)S(1)} fusion(f32[64,8,32,512]{3,2,1,0:T(8,128)S(1)} %copy.13), kind=kLoop, calls=%fused_computation | loop fusion | flops 8126464 | bytes 34603008 | tf_op jit(solution)/shard_map/reduce_sum | solution.py:9
  361.5 0.0 copy-done.3
  361.5 1.9 fusion.3
  363.4 15.7 %all-gather.9.cloned.1.call-done = f32[2048,512]{0,1:T(8,128)} async-done(((f32[2048,64]{0,1:T(8,128)}), f32[2048,512]{0,1:T(8,128)}) %all-gather.9.cloned.1.call-update) | async-done | bytes 4194320 | tf_op jit(solution)/shard_map/all_gather | solution.py:29
  379.1 10.8 %bitcast_subtract_fusion = f32[2048,512]{0,1:T(8,128)} fusion(f32[2048,512]{0,1:T(8,128)} %copy-done.2, f32[512,512]{1,0:T(8,128)S(1)} %fusion.3, f32[2048,512]{0,1:T(8,128)} %all-gather.9.cloned.1.call-done), kind=kOutput, calls=%fused_computation.2 | convolution fusion | flops 6443499520 | bytes 13631488 | tf_op jit(solution)/shard_map/dot_general | solution.py:13
  389.9 0.0 copy-start.1
  389.9 2.7 fusion.1
  392.6 5.3 %copy.11 = f32[2048,512]{1,0:T(8,128)} copy(f32[2048,512]{0,1:T(8,128)} %fusion.1) | data formatting | bytes 8388608 | tf_op jit(solution)/shard_map/scatter | solution.py:34
  397.9 0.0 copy-done.1
Async XLA Ops:
  6.5 168.8 %copy-start = (f32[512,512]{1,0:T(8,128)S(1)}, f32[512,512]{1,0:T(8,128)}, u32[]{:S(2)}) copy-start(f32[512,512]{1,0:T(8,128)} %param.10) | copy-start | bytes 3145732
  6.5 130.9 %all-gather.11.cloned.1.call-start = ((), (), s32[]{:S(2)}) async-start(), calls=%async_computation.2 | async-start | bytes 34603008 | tf_op jit(solution)/shard_map/all_gather | solution.py:9
  14.3 178.8 %all-gather.7.cloned.1.call-start = ((), (), s32[]{:S(2)}) async-start(), calls=%async_computation | async-start | bytes 4718592 | tf_op jit(solution)/shard_map/all_gather | solution.py:25
  15.0 308.6 %all-gather.13.cloned.1.call-start = ((), (), s32[]{:S(2)}) async-start(), calls=%async_computation.3 | async-start | bytes 34603008 | tf_op jit(solution)/shard_map/all_gather | solution.py:9
  202.5 2.0 copy-start.2
  205.6 173.5 %all-gather.9.cloned.1.call-start = ((), (), s32[]{:S(2)}) async-start(), calls=%async_computation.1 | async-start | bytes 4718592 | tf_op jit(solution)/shard_map/all_gather | solution.py:29
  356.1 5.4 %copy-start.3 = (f32[512,512]{1,0:T(8,128)S(1)}, f32[512,512]{1,0:T(8,128)}, u32[]{:S(2)}) copy-start(f32[512,512]{1,0:T(8,128)} %param.11) | copy-start | bytes 3145732
  389.9 8.0 %copy-start.1 = (f32[512,512]{1,0:T(8,128)S(1)}, f32[512,512]{1,0:T(8,128)}, u32[]{:S(2)}) copy-start(f32[512,512]{1,0:T(8,128)} %param.10) | copy-start | bytes 3145732
Sparse Core Ops, SparseCore 0:
  14.4 123.0 all-gather.10
  139.2 53.7 all-gather.6
  205.8 117.8 all-gather.12
  325.3 53.7 all-gather.8
